TPU v7x, 256 devices: a whole 4x4x8 slice. The times are simulated.
256 devices in a mesh: wide: 32 (over y, x, core), narrow: 8 (over z).
Axes of the slice: x: 4, y: 4, z: 8, core: 2. Of those that a mesh axis runs over, the one named last changes fastest.
Arguments:
- amplitudes: bfloat16 [1024, 16, 4096], P('wide', None, 'narrow'), may hold values from -6 to 6
- amp_tiles: int32 [32, 16], replicated, may hold values from 0 to 31, all different within a row
- integrals: bfloat16 [32, 2, 4096, 4096], P('wide', None, None, 'narrow'), may hold values from -0.09375 to 0.09375
- cd_tiles: int32 [32, 2], replicated, may hold values from 0 to 31, all different within a row
- q_owner: int32 [32], replicated, may hold values from 0 to 31, each once
Outputs:
- residual: bfloat16 [1024, 32, 4096], P('wide', None, 'narrow')
Inputs may be any that keep to these rules, and one draw needn't show every extreme that they name: `amp_tiles`: within a row, the 16 tiles are different. `cd_tiles`: within a row, the 2 tiles are different; every tile is named by some row. `q_owner`: each owner index appears once.
All inputs are finite; a program needn't handle non-finite values.
Results may differ from a plain program's by a relative error of at most 0.017.
Values may be sent and summed in bfloat16 or wider, within the bound.
A program may use at most 64 MiB of HBM per device.

v0:
```python
import jax
import jax.numpy as jnp
from jax import lax
from jax.sharding import PartitionSpec as P


def on_device(amplitudes, amp_tiles, integrals, cd_tiles, q_owner):
    my_index = lax.axis_index("wide")
    blocks = lax.axis_size("wide")
    rows_dev = amplitudes.shape[0]
    local_ints = integrals[0]
    tile_ids = jnp.arange(q_owner.shape[0], dtype=jnp.int32)
    holder = (q_owner[None, :] == jnp.arange(blocks, dtype=jnp.int32)[:, None]).astype(jnp.int32)
    owned_tile = jnp.sum(holder * tile_ids[None, :], axis=1)
    wanted = cd_tiles[owned_tile]
    my_wanted = wanted[my_index]
    segment = lax.all_gather(amplitudes, "wide", axis=0, tiled=True)
    length = segment.shape[0]
    source = jnp.arange(length, dtype=jnp.int32) // rows_dev
    tile_list = amp_tiles[source]
    picker = (tile_list[:, :, None] == my_wanted[None, None, :]).astype(jnp.bfloat16)
    chosen = jnp.einsum("rtk,rtc->rkc", picker, segment, preferred_element_type=jnp.float32).astype(
        jnp.bfloat16
    )
    partial_value = jnp.einsum(
        "rkc,kpc->rp", chosen, local_ints, preferred_element_type=jnp.float32
    )
    shares = lax.psum_scatter(
        partial_value.astype(jnp.bfloat16), "narrow", scatter_dimension=1, tiled=True
    )
    returned = lax.all_to_all(
        shares.reshape(blocks, rows_dev, shares.shape[1]),
        "wide",
        split_axis=0,
        concat_axis=0,
        tiled=True,
    )
    result = jnp.take(returned, q_owner, axis=0)
    return jnp.transpose(result, (1, 0, 2))


def solution(mesh):
    placed = (P("wide", None, "narrow"), P(), P("wide", None, None, "narrow"), P(), P())
    return jax.shard_map(
        on_device, mesh=mesh, in_specs=placed, out_specs=P("wide", None, "narrow"), check_vma=False
    )
```

profile of v0, /device:TPU:1, one launch (start us, length us, event | category | flops | bytes accessed | tf_op | source)
XLA Modules:
  0.0 242.8 jit_solution(6019152147181182622)
XLA Ops:
  6.5 0.0 all-gather.2.cloned.1.call-start
  6.5 0.7 all-gather.2.cloned.1.call-update
  7.3 0.0 reduce-scatter.2.cloned.1.call-start
  7.3 0.8 copy.16
  8.1 0.8 copy.15
  8.8 0.8 select_reduce_fusion
  9.6 0.6 gather_fusion.1
  10.2 2.8 %gather_fusion = s32[1024,16]{1,0:T(8,128)S(1)} fusion(s32[32,16]{1,0:T(8,128)S(1)} %copy.15, s32[1024]{0:T(1024)S(1)} %broadcast_clamp_fusion), kind=kCustom, calls=%fused_computation | custom fusion | bytes 135168 | tf_op jit(solution)/shard_map/gather | solution.py:20
  13.1 78.6 %all-gather.2.cloned.1.call-done = bf16[1024,16,512]{2,1,0:T(8,128)(2,1)} async-done(((bf16[32,16,512]{2,1,0:T(8,128)(2,1)}), bf16[1024,16,512]{2,1,0:T(8,128)(2,1)}) %all-gather.2.cloned.1.call-update) | async-done | bytes 16777232 | tf_op jit(solution)/shard_map/all_gather | solution.py:17
  91.7 8.6 %convolution_convert_fusion = bf16[1024,2,512]{2,1,0:T(2,128)(2,1)S(1)} fusion(bf16[1024,16,512]{2,1,0:T(8,128)(2,1)} %all-gather.2.cloned.1.call-done, s32[1024,16]{1,0:T(8,128)S(1)} %gather_fusion, s32[2]{0:T(128)S(1)} %dynamic-slice_bitcast_fusion), kind=kOutput, calls=%fused_computation.5 | convolution fusion | flops 34635776 | bytes 18939912 | tf_op jit(solution)/shard_map/rtk,rtc->rkc/dot_general | solution.py:22
  100.3 14.4 %bitcast_convert_fusion = bf16[1024,4096]{1,0:T(8,128)(2,1)} fusion(bf16[1,2,4096,512]{3,2,1,0:T(8,128)(2,1)} %param.7, bf16[1024,2,512]{2,1,0:T(2,128)(2,1)S(1)} %convolution_convert_fusion), kind=kOutput, calls=%fused_computation.3 | convolution fusion | flops 8594128896 | bytes 18874368 | tf_op jit(solution)/shard_map/rkc,kpc->rp/dot_general | solution.py:25
  114.6 0.0 copy-start
  114.7 0.0 reduce-scatter.2.cloned.1.call-update
  114.7 94.2 %reduce-scatter.2.cloned.1.call-done = bf16[1024,512]{1,0:T(8,128)(2,1)} async-done(((bf16[1024,4096]{1,0:T(8,128)(2,1)}), bf16[1024,512]{1,0:T(8,128)(2,1)}) %reduce-scatter.2.cloned.1.call-update) | async-done | bytes 1048592 | tf_op jit(solution)/shard_map/reduce_scatter | solution.py:28
  208.9 7.5 %all-to-all-start = ((bf16[32,32,512]{2,1,0:T(8,128)(2,1)}), bf16[32,32,512]{2,1,0:T(8,128)(2,1)S(1)}, u32[]{:S(2)}, u32[]{:S(2)}) async-start(bf16[32,32,512]{2,1,0:T(8,128)(2,1)} %bitcast.16), calls=%async_computation.1 | async-start | bytes 2097152 | tf_op jit(solution)/shard_map/all_to_all | solution.py:31
  216.4 0.0 copy-done
  216.5 17.1 %all-to-all-done = bf16[32,32,512]{2,1,0:T(8,128)(2,1)S(1)} async-done(((bf16[32,32,512]{2,1,0:T(8,128)(2,1)}), bf16[32,32,512]{2,1,0:T(8,128)(2,1)S(1)}, u32[]{:S(2)}, u32[]{:S(2)}) %all-to-all-start) | async-done | bytes 1048608 | tf_op jit(solution)/shard_map/all_to_all | solution.py:31
  233.6 0.6 gather_fusion.2
  234.2 0.2 select_bitcast_fusion
  234.4 1.5 copy.18
  (8 shorter events, 0.1 us)
Async XLA Ops:
  6.5 85.1 %all-gather.2.cloned.1.call-start = ((), (), s32[]{:S(2)}) async-start(), calls=%async_computation.2 | async-start | bytes 17301504 | tf_op jit(solution)/shard_map/all_gather | solution.py:17
  7.3 201.7 %reduce-scatter.2.cloned.1.call-start = ((), (), s32[]{:S(2)}) async-start(), calls=%async_computation.3 | async-start | bytes 9437184 | tf_op jit(solution)/shard_map/reduce_scatter | solution.py:28
  114.6 101.8 %copy-start = (s32[32]{0:T(128)S(1)}, s32[32]{0:T(128)}, u32[]{:S(2)}) copy-start(s32[32]{0:T(128)} %param.9) | copy-start | bytes 388
  208.9 24.7 %all-to-all-start = ((bf16[32,32,512]{2,1,0:T(8,128)(2,1)}), bf16[32,32,512]{2,1,0:T(8,128)(2,1)S(1)}, u32[]{:S(2)}, u32[]{:S(2)}) async-start(bf16[32,32,512]{2,1,0:T(8,128)(2,1)} %bitcast.16), calls=%async_computation.1 | async-start | bytes 2097152 | tf_op jit(solution)/shard_map/all_to_all | solution.py:31
Sparse Core Ops, SparseCore 0:
  9.9 81.7 all-gather.1
  114.8 94.0 reduce-scatter.1
where the time goes:
time: 243 us
  waiting for transfers between devices  191 us (79%)
  matrix products  23 us (9%)
  between operations  13.5 us (6%)
  starting transfers between devices  7.52 us (3%)
  local copies, waits for them, and re-layouts  7.09 us (3%)
    reduce_scatter x1, waiting for transfers between devices, on_device(): lax.psum_scatter(partial_value.astype(jnp.bfloat16), 'narrow', scatter_di...  94.2 us
    all_gather x1, waiting for transfers between devices, on_device(): segment = lax.all_gather(amplitudes, 'wide', axis=0, tiled=True)  78.6 us
    all_to_all x1, waiting for transfers between devices, on_device(): lax.all_to_all(shares.reshape(blocks, rows_dev, shares.shape[1]), 'wide',...  17.1 us
    dot_general x1, matrix products, on_device(): jnp.einsum('rkc,kpc->rp', chosen, local_ints, preferred_element_type=jnp....  14.4 us
    dot_general x1, matrix products, on_device(): jnp.einsum('rtk,rtc->rkc', picker, segment, preferred_element_type=jnp.fl...  8.62 us
    all_to_all x1, starting transfers between devices, on_device(): lax.all_to_all(shares.reshape(blocks, rows_dev, shares.shape[1]), 'wide',...  7.48 us
  transfers between devices with their start and end apart: 3, of which 3 were waited for; matrix products, arithmetic and copies ran while one was open for 2% of the time, Pallas kernels for 0%

commit v1 on v0

v1 whole, which is shorter than its diff:
```python
import functools

import jax
import jax.numpy as jnp
from jax import lax
from jax.experimental import pallas as pl
from jax.experimental.pallas import tpu as pltpu
from jax.sharding import PartitionSpec as P

MESH = pl.DeviceIdType.MESH
F32, BF16, I32 = jnp.float32, jnp.bfloat16, jnp.int32

NB = 32
RB = 32
TW = 16
KV = 2
NZ = 8
W = 512
BPC = 4
NC = NB // BPC
R = BPC * RB
H = R // 2
SX, SY = 4, 4


def offset(slot):
    chip = slot // 2
    return chip // SX, chip % SX, slot % 2


def shifted(y, x, core, slot, sign):
    dy, dx, dc = offset(slot)
    if sign < 0:
        dy, dx = SY - dy, SX - dx
    return (lax.rem(y + dy, SY) * SX + lax.rem(x + dx, SX)) * 2 + lax.rem(core + dc, 2)


def dot(a, b):
    return lax.dot_general(a, b, (((1,), (0,)), ((), ())), preferred_element_type=F32)


def dot_t(a, b):
    return lax.dot_general(a, b, (((1,), (1,)), ((), ())), preferred_element_type=F32)


def kernel(
    amp_tiles, cd_tiles, q_owner, amp_hbm, ints_hbm, out_hbm,
    amp, ints, wanted, owner_rows, tile_lanes, amp_out, amp_in, first, right_in, left_in, fin_out, fin_in, out,
    load_sem, amp_send, amp_recv, right_send, right_recv, left_send, left_recv, fin_send, fin_recv,
):
    me = lax.axis_index("wide")
    z = lax.axis_index("narrow")
    core, x, y = lax.rem(me, 2), lax.rem(me // 2, SX), me // (2 * SX)
    z_right, z_left = lax.rem(z + 1, NZ), lax.rem(z + NZ - 1, NZ)

    load_amp = pltpu.make_async_copy(amp_hbm, amp, load_sem.at[0])
    load_ints = pltpu.make_async_copy(ints_hbm, ints, load_sem.at[1])
    load_amp.start()
    load_ints.start()

    barrier = pltpu.get_barrier_semaphore()
    for slot in range(1, NB):
        pl.semaphore_signal(barrier, inc=1, device_id=(shifted(y, x, core, slot, 1), z), device_id_type=MESH)
    for there in (z_right, z_left):
        pl.semaphore_signal(barrier, inc=1, device_id=(me, there), device_id_type=MESH)

    rows = lax.broadcasted_iota(I32, (NB, 128), 0)
    lanes = lax.broadcasted_iota(I32, (1, 128), 1)
    owners = jnp.zeros((NB, 128), I32)
    wants = [jnp.zeros((NB, 128), I32) for _ in range(KV)]
    for q in range(NB):
        owner = q_owner[q]
        owners = jnp.where(rows == q, owner, owners)
        for k in range(KV):
            wants[k] = jnp.where(rows == owner, cd_tiles[k, q], wants[k])
    owner_rows[...] = owners
    for k in range(KV):
        wanted[k] = wants[k]
    held = jnp.zeros((1, 128), I32)
    for t in range(TW):
        held = jnp.where(lax.rem(lanes, TW) == t, amp_tiles[t, me], held)
    tile_lanes[...] = jnp.broadcast_to(held, (8, 128))

    def amp_copy(slot):
        return pltpu.make_async_remote_copy(
            src_ref=amp_out.at[slot], dst_ref=amp_in.at[slot], send_sem=amp_send.at[slot], recv_sem=amp_recv.at[slot],
            device_id=(shifted(y, x, core, slot, 1), z), device_id_type=MESH)

    def fin_copy(slot):
        return pltpu.make_async_remote_copy(
            src_ref=fin_out.at[slot], dst_ref=fin_in.at[slot], send_sem=fin_send.at[slot], recv_sem=fin_recv.at[slot],
            device_id=(shifted(y, x, core, slot, -1), z), device_id_type=MESH)

    def right_copy(step, chunk):
        if step == 0:
            src, dst = first.at[chunk, pl.ds(0, H)], right_in.at[0, chunk, pl.ds(0, H)]
        else:
            src, dst = right_in.at[step - 1, chunk], right_in.at[step, chunk]
        return pltpu.make_async_remote_copy(
            src_ref=src, dst_ref=dst, send_sem=right_send.at[step, chunk], recv_sem=right_recv.at[step, chunk],
            device_id=(me, z_right), device_id_type=MESH)

    def left_copy(step, chunk):
        if step == 0:
            src, dst = first.at[chunk, pl.ds(H, H)], left_in.at[0, chunk, pl.ds(H, H)]
        else:
            src, dst = left_in.at[step - 1, chunk], left_in.at[step, chunk]
        return pltpu.make_async_remote_copy(
            src_ref=src, dst_ref=dst, send_sem=left_send.at[step, chunk], recv_sem=left_recv.at[step, chunk],
            device_id=(me, z_left), device_id_type=MESH)

    load_amp.wait()
    pl.semaphore_wait(barrier, NB - 1 + 2)

    spread_rows = lax.broadcasted_iota(I32, (RB, RB * TW), 0)
    spread_lanes = lax.broadcasted_iota(I32, (RB, RB * TW), 1)
    spread = jnp.where(spread_lanes // TW == spread_rows, 1.0, 0.0)

    @pl.loop(0, NC)
    def _(chunk):
        pieces = []
        for u in range(BPC):
            there = shifted(y, x, core, chunk * BPC + u, 1)
            for k in range(KV):
                hit = jnp.where(tile_lanes[pl.ds(0, 1), :] == wanted[k, pl.ds(there, 1), :], 1.0, 0.0)
                hit = jnp.concatenate([hit] * (RB * TW // 128), axis=1)
                pieces.append((spread * hit).astype(BF16))
        picked = dot(jnp.concatenate(pieces, axis=0), amp[...]).astype(BF16)
        amp_out[pl.ds(chunk * BPC, BPC)] = picked.reshape(BPC, KV, RB, W)

        @pl.when(chunk == 0)
        def _():
            amp_in[0] = picked[: KV * RB].reshape(KV, RB, W)

        for u in range(BPC):
            @pl.when(chunk * BPC + u > 0)
            def _():
                amp_copy(chunk * BPC + u).start()

    load_ints.wait()

    def term(chunk, part):
        total = None
        for k in range(KV):
            left = amp_in[pl.ds(chunk * BPC, BPC), k].reshape(R, W)
            value = dot_t(left, ints[k, part])
            total = value if total is None else total + value
        return total

    @pl.loop(0, NC + 5)
    def _(t):
        @pl.when(t < NC)
        def _():
            for u in range(BPC):
                @pl.when(t * BPC + u > 0)
                def _():
                    amp_copy(t * BPC + u).wait_recv()
            first[t] = term(t, lax.rem(z + 4, NZ)).astype(BF16)
            right_copy(0, t).start()
            left_copy(0, t).start()

        for step in range(1, 4):
            chunk = t - step

            @pl.when((chunk >= 0) & (chunk < NC))
            def _():
                value = term(chunk, lax.rem(z + 4 - step, NZ))
                right_copy(step - 1, chunk).wait_recv()
                if step == 1:
                    right_in[0, chunk, :H] = (value[:H] + right_in[0, chunk, :H].astype(F32)).astype(BF16)
                    right_in[0, chunk, H:] = value[H:].astype(BF16)
                else:
                    right_in[step - 1, chunk] = (value + right_in[step - 1, chunk].astype(F32)).astype(BF16)
                right_copy(step, chunk).start()
                value = term(chunk, lax.rem(z + NZ - 4 + step, NZ))
                left_copy(step - 1, chunk).wait_recv()
                if step == 1:
                    left_in[0, chunk, :H] = value[:H].astype(BF16)
                    left_in[0, chunk, H:] = (value[H:] + left_in[0, chunk, H:].astype(F32)).astype(BF16)
                else:
                    left_in[step - 1, chunk] = (value + left_in[step - 1, chunk].astype(F32)).astype(BF16)
                left_copy(step, chunk).start()

        last = t - 4

        @pl.when((last >= 0) & (last < NC))
        def _():
            value = term(last, z)
            right_copy(3, last).wait_recv()
            left_copy(3, last).wait_recv()
            value = value + right_in[3, last].astype(F32) + left_in[3, last].astype(F32)
            done = value.astype(BF16).reshape(BPC, RB, W)
            fin_out[pl.ds(last * BPC, BPC)] = done

            @pl.when(last == 0)
            def _():
                fin_in[0] = done[0]

            for u in range(BPC):
                @pl.when(last * BPC + u > 0)
                def _():
                    fin_copy(last * BPC + u).start()

        back = t - 5

        @pl.when(back >= 0)
        def _():
            source = jnp.zeros((1, 128), I32)
            for u in range(BPC):
                source = jnp.where(lanes // RB == u, shifted(y, x, core, back * BPC + u, 1), source)
            match = jnp.where(owner_rows[...] == source, 1.0, 0.0)
            for u in range(BPC):
                @pl.when(back * BPC + u > 0)
                def _():
                    fin_copy(back * BPC + u).wait_recv()
            values = fin_in[pl.ds(back * BPC, BPC)].reshape(R, W)
            for r in range(0, RB, 4):
                place = jnp.concatenate([jnp.where(lax.rem(lanes, RB) == r + i, match, 0.0) for i in range(4)], axis=0)
                moved = dot(place.astype(BF16), values)
                span = pl.ds(r * NB, 4 * NB)

                @pl.when(back == 0)
                def _():
                    out[span, :] = moved.astype(BF16)

                @pl.when(back > 0)
                def _():
                    out[span, :] = (moved + out[span, :].astype(F32)).astype(BF16)

    store = pltpu.make_async_copy(out, out_hbm, load_sem.at[2])
    store.start()

    @pl.loop(1, NB)
    def _(slot):
        amp_copy(slot).wait_send()
        fin_copy(slot).wait_send()

    @pl.loop(0, NC)
    def _(chunk):
        for step in range(4):
            right_copy(step, chunk).wait_send()
            left_copy(step, chunk).wait_send()

    store.wait()


def on_device(amplitudes, amp_tiles, integrals, cd_tiles, q_owner):
    any_space = pl.BlockSpec(memory_space=pl.ANY)
    smem = pl.BlockSpec(memory_space=pltpu.SMEM)
    dma = pltpu.SemaphoreType.DMA
    result = pl.pallas_call(
        kernel,
        out_shape=jax.ShapeDtypeStruct((RB * NB, W), BF16),
        in_specs=[smem, smem, smem, any_space, any_space],
        out_specs=any_space,
        scratch_shapes=[
            pltpu.VMEM((RB * TW, W), BF16),
            pltpu.VMEM((KV, NZ, W, W), BF16),
            pltpu.VMEM((KV, NB, 128), I32),
            pltpu.VMEM((NB, 128), I32),
            pltpu.VMEM((8, 128), I32),
            pltpu.VMEM((NB, KV, RB, W), BF16),
            pltpu.VMEM((NB, KV, RB, W), BF16),
            pltpu.VMEM((NC, R, W), BF16),
            pltpu.VMEM((4, NC, R, W), BF16),
            pltpu.VMEM((4, NC, R, W), BF16),
            pltpu.VMEM((NB, RB, W), BF16),
            pltpu.VMEM((NB, RB, W), BF16),
            pltpu.VMEM((RB * NB, W), BF16),
            dma((3,)), dma((NB,)), dma((NB,)),
            dma((4, NC)), dma((4, NC)), dma((4, NC)), dma((4, NC)),
            dma((NB,)), dma((NB,)),
        ],
        compiler_params=pltpu.CompilerParams(
            collective_id=0, has_side_effects=True, vmem_limit_bytes=56 * 1024 * 1024),
        name="ladder",
    )(amp_tiles.T, cd_tiles.T, q_owner, amplitudes.reshape(RB * TW, W), integrals.reshape(KV, NZ, W, W))
    return result.reshape(RB, NB, W)


def solution(mesh):
    placed = (P("wide", None, "narrow"), P(), P("wide", None, None, "narrow"), P(), P())
    return jax.shard_map(
        on_device, mesh=mesh, in_specs=placed, out_specs=P("wide", None, "narrow"), check_vma=False
    )
```

time: 243 us -> 116 us (0.48)
  waiting for transfers between devices: 191 us -> 0 us
  Pallas kernels: 0 us -> 113 us
  matrix products: 23 us -> 0 us
  between operations: 13.5 us -> 0.01 us
  starting transfers between devices: 7.52 us -> 0 us
  local copies, waits for them, and re-layouts: 7.09 us -> 2.3 us
    pallas_call x0 -> x1, Pallas kernels: none -> 113 us  [on_device(): pl.pallas_call(kernel, out_shape=jax.ShapeDtypeStruct((RB * NB, W), BF16)...]
    reduce_scatter x1 -> x0, waiting for transfers between devices: 94.2 us -> none  [on_device(): lax.psum_scatter(partial_value.astype(jnp.bfloat16), 'narrow', scatter_di...]
    all_gather x1 -> x0, waiting for transfers between devices: 78.6 us -> none  [on_device(): segment = lax.all_gather(amplitudes, 'wide', axis=0, tiled=True)]
    dot_general x2 -> x0, matrix products: 23 us -> none  [the longest x1 14.4 us: on_device(): jnp.einsum('rkc,kpc->rp', chosen, local_ints, preferred_element_type=jnp....]
    all_to_all x1 -> x0, waiting for transfers between devices: 17.1 us -> none  [on_device(): lax.all_to_all(shares.reshape(blocks, rows_dev, shares.shape[1]), 'wide',...]
    all_to_all x1 -> x0, starting transfers between devices: 7.48 us -> none  [on_device(): lax.all_to_all(shares.reshape(blocks, rows_dev, shares.shape[1]), 'wide',...]
    gather x3 -> x0, local copies, waits for them, and re-layouts: 4 us -> none  [the longest x1 2.81 us: on_device(): tile_list = amp_tiles[source]]
  transfers between devices with their start and end apart: 3 -> 0, of which waited for: 3 -> 0; matrix products, arithmetic and copies ran while one was open for 2% -> 0% of each run, Pallas kernels for 0% -> 0%
where the time goes in v1:
time: 116 us; the launch traced here: 115 us
  Pallas kernels  113 us (97%)
  local copies, waits for them, and re-layouts  2.3 us (2%)
    pallas_call x1, Pallas kernels, on_device(): pl.pallas_call(kernel, out_shape=jax.ShapeDtypeStruct((RB * NB, W), BF16)...  113 us

profile of v1, /device:TPU:1, one launch (start us, length us, event | category | flops | bytes accessed | tf_op | source)
XLA Modules:
  0.0 115.0 jit_solution(2845687079900906310)
XLA Ops:
  0.0 112.7 %ladder.1 = bf16[1024,512]{1,0:T(8,128)(2,1)} custom-call(s32[16,32]{1,0:T(8,128)} %bitcast.8, s32[2,32]{1,0:T(2,128)} %bitcast.9, s32[32]{0:T(128)} %q_owner.1, bf16[512,512]{1,0:T(8,128)(2,1)} %bitcast.7, bf16[2,8,512,512]{3,2,1,0:T(8,128)(2,1)} %bitcast.5), custom_call_target="tpu_custom_call" | custom-call | tf_op jit(solution)/shard_map/ladder/pallas_call | solution.py:251
  112.7 2.3 %copy.7 = bf16[32,32,512]{2,1,0:T(8,128)(2,1)} copy(bf16[32,32,512]{2,1,0:T(8,128)(2,1)} %bitcast.6) | data formatting | bytes 2097152

commit v2 on v1

v2 whole, which is shorter than its diff:
```python
import jax
import jax.numpy as jnp
from jax import lax
from jax.experimental import pallas as pl
from jax.experimental.pallas import tpu as pltpu
from jax.sharding import PartitionSpec as P

MESH = pl.DeviceIdType.MESH
F32, BF16, I32 = jnp.float32, jnp.bfloat16, jnp.int32

NB = 32
RB = 32
TW = 16
KV = 2
NZ = 8
W = 512
SX, SY = 4, 4
CHIPS = [(0, 1), (0, 3), (1, 0), (1, 1), (3, 3), (1, 3), (3, 1), (0, 2), (2, 0), (2, 1), (2, 3), (1, 2), (3, 2), (2, 2), (3, 0)]
NC = len(CHIPS) + 2
AHEAD = 4


def digits(values):
    code = sum(v << (2 * i) for i, v in enumerate(values))
    return code - (1 << 32) if code >= 1 << 31 else code


DY, DX = digits([0] + [c[0] for c in CHIPS]), digits([0] + [c[1] for c in CHIPS])


def offset(slot):
    if isinstance(slot, int):
        return (*((0, 0) if slot in (0, NB - 1) else CHIPS[(slot - 1) // 2]), (slot + 1) % 2 if 0 < slot < NB - 1 else slot % 2)
    at = 2 * lax.rem((slot + 1) // 2, 16)
    last = slot // (NB - 1)
    core = jnp.where(slot == 0, 0, lax.rem(slot + 1 + last, 2))
    return lax.shift_right_logical(jnp.int32(DY), at) & 3, lax.shift_right_logical(jnp.int32(DX), at) & 3, core


def shifted(y, x, core, slot, sign):
    dy, dx, dc = offset(slot)
    if sign < 0:
        dy, dx = SY - dy, SX - dx
    return (lax.rem(y + dy, SY) * SX + lax.rem(x + dx, SX)) * 2 + lax.rem(core + dc, 2)


def by_size(chunk, run):
    edge = (chunk == 0) | (chunk == NC - 1)

    @pl.when(edge)
    def _():
        run(chunk // (NC - 1) * (NB - 1), 1)

    @pl.when((chunk > 0) & (chunk < NC - 1))
    def _():
        run(2 * chunk - 1, 2)


def rows_of(slot, blocks):
    return pl.ds(pl.multiple_of(slot * RB, RB), blocks * RB)


def halves_of(slot, blocks):
    half = blocks * RB // 2
    start = pl.multiple_of(slot * RB, RB)
    return pl.ds(start, half), pl.ds(pl.multiple_of(start + half, 16), half)


def dot(a, b):
    return lax.dot_general(a, b, (((1,), (0,)), ((), ())), preferred_element_type=F32)


def dot_t(a, b):
    return lax.dot_general(a, b, (((1,), (1,)), ((), ())), preferred_element_type=F32)


def kernel(
    amp_tiles, cd_tiles, q_owner, amp_hbm, ints_hbm, out,
    amp, ints, wanted, tile_lanes, amp_out, amp_in, first, right_in, left_in, fin_out,
    load_sem, ints_sem, amp_send, amp_recv, right_send, right_recv, left_send, left_recv, fin_send, fin_recv,
):
    me = lax.axis_index("wide")
    z = lax.axis_index("narrow")
    core, x, y = lax.rem(me, 2), lax.rem(me // 2, SX), me // (2 * SX)
    z_right, z_left = lax.rem(z + 1, NZ), lax.rem(z + NZ - 1, NZ)

    def ints_copy(part):
        return pltpu.make_async_copy(ints_hbm.at[:, part], ints.at[:, part], ints_sem.at[part])

    load_amp = pltpu.make_async_copy(amp_hbm, amp, load_sem.at[0])
    load_amp.start()
    ints_copy(lax.rem(z + 4, NZ)).start()

    barrier = pltpu.get_barrier_semaphore()
    for slot in range(1, NB):
        pl.semaphore_signal(barrier, inc=1, device_id=(shifted(y, x, core, slot, 1), z), device_id_type=MESH)
    for there in (z_right, z_left):
        pl.semaphore_signal(barrier, inc=1, device_id=(me, there), device_id_type=MESH)

    rows = lax.broadcasted_iota(I32, (NB, 128), 0)
    lanes = lax.broadcasted_iota(I32, (1, 128), 1)
    wants = [jnp.zeros((NB, 128), I32) for _ in range(KV)]
    for q in range(NB):
        owner = q_owner[q]
        for k in range(KV):
            wants[k] = jnp.where(rows == owner, cd_tiles[k, q], wants[k])
    for k in range(KV):
        wanted[k] = wants[k]
    held = jnp.zeros((1, 128), I32)
    for t in range(TW):
        held = jnp.where(lax.rem(lanes, TW) == t, amp_tiles[t, me], held)
    tile_lanes[...] = jnp.broadcast_to(held, (8, 128))
    for distance in (3, 5, 2, 6, 1, 7, 0):
        ints_copy(lax.rem(z + distance, NZ)).start()

    def amp_copy(slot):
        return pltpu.make_async_remote_copy(
            src_ref=amp_out.at[slot], dst_ref=amp_in.at[slot], send_sem=amp_send.at[slot], recv_sem=amp_recv.at[slot],
            device_id=(shifted(y, x, core, slot, 1), z), device_id_type=MESH)

    def fin_copy(slot):
        return pltpu.make_async_remote_copy(
            src_ref=fin_out.at[rows_of(slot, 1)], dst_ref=out.at[me], send_sem=fin_send.at[slot],
            recv_sem=fin_recv.at[slot], device_id=(shifted(y, x, core, slot, -1), z), device_id_type=MESH)

    def ring_copy(held, sends, recvs, there, side, step, chunk, slot, blocks):
        if step == 0:
            span = halves_of(slot, blocks)[side]
            src, dst = first.at[span], held.at[0, span]
        else:
            span = rows_of(slot, blocks)
            src, dst = held.at[step - 1, span], held.at[step, span]
        return pltpu.make_async_remote_copy(
            src_ref=src, dst_ref=dst, send_sem=sends.at[step, chunk], recv_sem=recvs.at[step, chunk],
            device_id=(me, there), device_id_type=MESH)

    def right_copy(*where):
        return ring_copy(right_in, right_send, right_recv, z_right, 0, *where)

    def left_copy(*where):
        return ring_copy(left_in, left_send, left_recv, z_left, 1, *where)

    own_rows = pltpu.make_async_copy(fin_out.at[pl.ds(0, RB)], out.at[me], load_sem.at[1])
    load_amp.wait()

    spread_rows = lax.broadcasted_iota(I32, (RB, RB * TW), 0)
    spread_lanes = lax.broadcasted_iota(I32, (RB, RB * TW), 1)
    spread = jnp.where(spread_lanes // TW == spread_rows, 1.0, 0.0)

    def pick(slot, blocks):
        pieces = []
        for u in range(blocks):
            there = shifted(y, x, core, slot + u, 1)
            for k in range(KV):
                hit = jnp.where(tile_lanes[pl.ds(0, 1), :] == wanted[k, pl.ds(there, 1), :], 1.0, 0.0)
                hit = jnp.concatenate([hit] * (RB * TW // 128), axis=1)
                pieces.append((spread * hit).astype(BF16))
        picked = dot(jnp.concatenate(pieces, axis=0), amp[...]).astype(BF16)
        return picked.reshape(blocks, KV, RB, W)

    def send_amplitudes(slot, blocks):
        amp_out[pl.ds(slot, blocks)] = pick(slot, blocks)
        for u in range(blocks):
            amp_copy(slot + u).start()

    amp_in[0] = pick(0, 1)[0]
    pl.semaphore_wait(barrier, NB - 1 + 2)

    @pl.loop(1, AHEAD)
    def _(chunk):
        send_amplitudes(2 * chunk - 1, 2)

    def term(slot, blocks, part):
        total = None
        for k in range(KV):
            left = amp_in[pl.ds(slot, blocks), k].reshape(blocks * RB, W)
            value = dot_t(left, ints[k, part])
            total = value if total is None else total + value
        return total

    @pl.loop(0, NC + 4)
    def _(t):
        def start(slot, blocks):
            for u in range(blocks):
                @pl.when(slot + u > 0)
                def _():
                    amp_copy(slot + u).wait_recv()

            if blocks == 1:
                @pl.when(slot == 0)
                def _():
                    ints_copy(lax.rem(z + 4, NZ)).wait()
            first[rows_of(slot, blocks), :] = term(slot, blocks, lax.rem(z + 4, NZ)).astype(BF16)
            right_copy(0, t, slot, blocks).start()
            left_copy(0, t, slot, blocks).start()

        @pl.when(t < NC)
        def _():
            by_size(t, start)

        @pl.when(2 * t < NC - 1 - AHEAD)
        def _():
            send_amplitudes(2 * (AHEAD + 2 * t) - 1, 2)

        @pl.when(2 * t + 1 < NC - 1 - AHEAD)
        def _():
            send_amplitudes(2 * (AHEAD + 2 * t) + 1, 2)

        @pl.when(2 * t == NC - 1 - AHEAD + (NC - 1 - AHEAD) % 2)
        def _():
            send_amplitudes(NB - 1, 1)

        for step in range(1, 4):
            chunk = t - step

            def move(slot, blocks):
                if blocks == 1:
                    @pl.when(slot == 0)
                    def _():
                        ints_copy(lax.rem(z + 4 - step, NZ)).wait()
                        ints_copy(lax.rem(z + NZ - 4 + step, NZ)).wait()

                everything = rows_of(slot, blocks)
                half = blocks * RB // 2
                spans = halves_of(slot, blocks)
                for side, (held, copy, part) in enumerate((
                    (right_in, right_copy, lax.rem(z + 4 - step, NZ)),
                    (left_in, left_copy, lax.rem(z + NZ - 4 + step, NZ)),
                )):
                    value = term(slot, blocks, part)
                    copy(step - 1, chunk, slot, blocks).wait_recv()
                    if step == 1:
                        came, new = spans[side], spans[1 - side]
                        parts = (value[:half], value[half:])
                        held[0, came, :] = (parts[side] + held[0, came, :].astype(F32)).astype(BF16)
                        held[0, new, :] = parts[1 - side].astype(BF16)
                    else:
                        held[step - 1, everything, :] = (value + held[step - 1, everything, :].astype(F32)).astype(BF16)
                    copy(step, chunk, slot, blocks).start()

            @pl.when((chunk >= 0) & (chunk < NC))
            def _():
                by_size(chunk, move)

        last = t - 4

        def finish(slot, blocks):
            if blocks == 1:
                @pl.when(slot == 0)
                def _():
                    ints_copy(z).wait()

            everything = rows_of(slot, blocks)
            value = term(slot, blocks, z)
            right_copy(3, last, slot, blocks).wait_recv()
            left_copy(3, last, slot, blocks).wait_recv()
            value = value + right_in[3, everything, :].astype(F32) + left_in[3, everything, :].astype(F32)
            fin_out[everything, :] = value.astype(BF16)
            if blocks == 1:
                @pl.when(slot == 0)
                def _():
                    own_rows.start()
            for u in range(blocks):
                @pl.when(slot + u > 0)
                def _():
                    fin_copy(slot + u).start()

        @pl.when(last >= 0)
        def _():
            by_size(last, finish)

    own_rows.wait()

    @pl.loop(1, NB)
    def _(slot):
        amp_copy(slot).wait_send()
        fin_copy(slot).wait()

    @pl.loop(0, NC)
    def _(chunk):
        def drain(slot, blocks):
            for step in range(4):
                right_copy(step, chunk, slot, blocks).wait_send()
                left_copy(step, chunk, slot, blocks).wait_send()

        by_size(chunk, drain)


def on_device(amplitudes, amp_tiles, integrals, cd_tiles, q_owner):
    any_space = pl.BlockSpec(memory_space=pl.ANY)
    smem = pl.BlockSpec(memory_space=pltpu.SMEM)
    dma = pltpu.SemaphoreType.DMA
    result = pl.pallas_call(
        kernel,
        out_shape=jax.ShapeDtypeStruct((NB, RB, W), BF16),
        in_specs=[smem, smem, smem, any_space, any_space],
        out_specs=any_space,
        scratch_shapes=[
            pltpu.VMEM((RB * TW, W), BF16),
            pltpu.VMEM((KV, NZ, W, W), BF16),
            pltpu.VMEM((KV, NB, 128), I32),
            pltpu.VMEM((8, 128), I32),
            pltpu.VMEM((NB, KV, RB, W), BF16),
            pltpu.VMEM((NB, KV, RB, W), BF16),
            pltpu.VMEM((NB * RB, W), BF16),
            pltpu.VMEM((4, NB * RB, W), BF16),
            pltpu.VMEM((4, NB * RB, W), BF16),
            pltpu.VMEM((NB * RB, W), BF16),
            dma((2,)), dma((NZ,)), dma((NB,)), dma((NB,)),
            dma((4, NC)), dma((4, NC)), dma((4, NC)), dma((4, NC)),
            dma((NB,)), dma((NB,)),
        ],
        compiler_params=pltpu.CompilerParams(
            collective_id=0, has_side_effects=True, vmem_limit_bytes=56 * 1024 * 1024),
        name="ladder",
    )(amp_tiles.T, cd_tiles.T, q_owner, amplitudes.reshape(RB * TW, W), integrals.reshape(KV, NZ, W, W))
    return jnp.transpose(jnp.take(result, q_owner, axis=0, mode="clip"), (1, 0, 2))


def solution(mesh):
    placed = (P("wide", None, "narrow"), P(), P("wide", None, None, "narrow"), P(), P())
    return jax.shard_map(
        on_device, mesh=mesh, in_specs=placed, out_specs=P("wide", None, "narrow"), check_vma=False
    )
```

time: 116 us -> 111 us (0.957)
  Pallas kernels: 113 us -> 107 us
    pallas_call x1, Pallas kernels: 113 us -> 107 us  [on_device(): pl.pallas_call(kernel, out_shape=jax.ShapeDtypeStruct((NB, RB, W), BF16),...]
    unnamed x1 -> x0, local copies, waits for them, and re-layouts: 2.3 us -> none
    gather x0 -> x1, local copies, waits for them, and re-layouts: none -> 1.84 us  [on_device(): jnp.take(result, q_owner, axis=0, mode='clip')]
    transpose x0 -> x1, local copies, waits for them, and re-layouts: none -> 1.55 us  [on_device(): jnp.transpose(jnp.take(result, q_owner, axis=0, mode='clip'), (1, 0, 2))]
where the time goes in v2:
time: 111 us
  Pallas kernels  107 us (96%)
  local copies, waits for them, and re-layouts  3.39 us (3%)
    pallas_call x1, Pallas kernels, on_device(): pl.pallas_call(kernel, out_shape=jax.ShapeDtypeStruct((NB, RB, W), BF16),...  107 us

profile of v2, /device:TPU:1, one launch (start us, length us, event | category | flops | bytes accessed | tf_op | source)
XLA Modules:
  0.0 111.1 jit_solution(10417277855062328204)
XLA Ops:
  0.0 0.7 pad_clamp_fusion
  0.7 107.0 %ladder.1 = bf16[32,32,512]{2,1,0:T(8,128)(2,1)} custom-call(s32[16,32]{1,0:T(8,128)} %bitcast.8, s32[2,32]{1,0:T(2,128)} %bitcast.9, s32[32]{0:T(128)} %q_owner.1, bf16[512,512]{1,0:T(8,128)(2,1)} %bitcast.7, bf16[2,8,512,512]{3,2,1,0:T(8,128)(2,1)} %bitcast.5), custom_call_target="tpu_custom_call" | custom-call | tf_op jit(solution)/shard_map/ladder/pallas_call | solution.py:293
  107.7 1.8 %gather_fusion = bf16[32,32,512]{2,1,0:T(8,128)(2,1)S(1)} fusion(bf16[32,32,512]{2,1,0:T(8,128)(2,1)} %ladder.1, s32[1024]{0:T(1024)S(1)} %pad_clamp_fusion), kind=kCustom, calls=%fused_computation | custom fusion | bytes 2097280 | tf_op jit(solution)/shard_map/jit(_take)/gather | solution.py:317
  109.5 1.5 %copy.6 = bf16[32,32,512]{2,1,0:T(8,128)(2,1)} copy(bf16[32,32,512]{2,0,1:T(8,128)(2,1)S(1)} %bitcast.6) | data formatting | bytes 2097152 | tf_op jit(solution)/shard_map/transpose | solution.py:317

commit v3 on v1

v3 whole, which is shorter than its diff:
```python
import functools

import jax
import jax.numpy as jnp
from jax import lax
from jax.experimental import pallas as pl
from jax.experimental.pallas import tpu as pltpu
from jax.sharding import PartitionSpec as P

MESH = pl.DeviceIdType.MESH
F32, BF16, I32 = jnp.float32, jnp.bfloat16, jnp.int32

NB = 32
RB = 32
TW = 16
KV = 2
NZ = 8
W = 512
BPC = 2
NC = NB // BPC
R = BPC * RB
H = R // 2
PW = 256
STRIDE = 40
SX, SY = 4, 4
AHEAD = 4
SINGLE = 2
CHIPS = [(0, 0), (0, 1), (0, 3), (1, 0), (1, 1), (3, 3), (1, 3), (3, 1), (0, 2), (2, 0), (2, 1), (2, 3), (1, 2), (3, 2), (2, 2), (3, 0)]


def digits(values):
    code = sum(v << (2 * i) for i, v in enumerate(values))
    return code - (1 << 32) if code >= 1 << 31 else code


DY, DX = digits([c[0] for c in CHIPS]), digits([c[1] for c in CHIPS])


def offset(slot):
    chip = slot // 2
    if isinstance(slot, int):
        return (*CHIPS[chip], slot % 2)
    at = 2 * chip
    return lax.shift_right_logical(jnp.int32(DY), at) & 3, lax.shift_right_logical(jnp.int32(DX), at) & 3, slot % 2


def shifted(y, x, core, slot, sign):
    dy, dx, dc = offset(slot)
    if sign < 0:
        dy, dx = SY - dy, SX - dx
    return (lax.rem(y + dy, SY) * SX + lax.rem(x + dx, SX)) * 2 + lax.rem(core + dc, 2)


def dot(a, b):
    return lax.dot_general(a, b, (((1,), (0,)), ((), ())), preferred_element_type=F32)


def dot_t(a, b):
    return lax.dot_general(a, b, (((1,), (1,)), ((), ())), preferred_element_type=F32)


def kernel(
    tiles_hbm, cd_hbm, owner_hbm, amp_hbm, ints_hbm, out,
    amp_tiles, cd_tiles, q_owner,
    amp, ints, wanted, tile_lanes, amp_out, amp_in, first, own, right_in, left_in, fin_out,
    load_sem, ints_sem, amp_send, amp_recv, right_send, right_recv, left_send, left_recv, fin_send, fin_recv,
):
    me = lax.axis_index("wide")
    z = lax.axis_index("narrow")
    core, x, y = lax.rem(me, 2), lax.rem(me // 2, SX), me // (2 * SX)
    z_right, z_left = lax.rem(z + 1, NZ), lax.rem(z + NZ - 1, NZ)

    def ints_copy(part):
        return pltpu.make_async_copy(ints_hbm.at[:, part], ints.at[:, part], ints_sem.at[part])

    load_amp = pltpu.make_async_copy(amp_hbm, amp, load_sem.at[0])
    load_tables = [
        pltpu.make_async_copy(src, dst, load_sem.at[2 + i])
        for i, (src, dst) in enumerate(((tiles_hbm, amp_tiles), (cd_hbm, cd_tiles), (owner_hbm, q_owner)))
    ]
    for load in load_tables:
        load.start()
    load_amp.start()
    ints_copy(lax.rem(z + 4, NZ)).start()

    barrier = pltpu.get_barrier_semaphore()
    for slot in range(1, NB):
        pl.semaphore_signal(barrier, inc=1, device_id=(shifted(y, x, core, slot, 1), z), device_id_type=MESH)
    for there in (z_right, z_left):
        pl.semaphore_signal(barrier, inc=1, device_id=(me, there), device_id_type=MESH)

    for load in load_tables:
        load.wait()
    rows = lax.broadcasted_iota(I32, (NB, 128), 0)
    lanes = lax.broadcasted_iota(I32, (1, 128), 1)
    wants = [jnp.zeros((NB, 128), I32) for _ in range(KV)]
    for q in range(NB):
        owner = q_owner[q]
        for k in range(KV):
            wants[k] = jnp.where(rows == owner, cd_tiles[k, q], wants[k])
    for k in range(KV):
        wanted[k] = wants[k]
    held = jnp.zeros((1, 128), I32)
    for t in range(TW):
        held = jnp.where(lax.rem(lanes, TW) == t, amp_tiles[t, me], held)
    tile_lanes[...] = jnp.broadcast_to(held, (8, 128))

    def amp_copy(slot):
        return pltpu.make_async_remote_copy(
            src_ref=amp_out.at[slot], dst_ref=amp_in.at[slot], send_sem=amp_send.at[slot], recv_sem=amp_recv.at[slot],
            device_id=(shifted(y, x, core, slot, 1), z), device_id_type=MESH)

    def fin_copy(slot):
        return pltpu.make_async_remote_copy(
            src_ref=fin_out.at[slot], dst_ref=out.at[me], send_sem=fin_send.at[slot], recv_sem=fin_recv.at[slot],
            device_id=(shifted(y, x, core, slot, -1), z), device_id_type=MESH)

    def right_copy(step, chunk):
        if step == 0:
            src, dst = first.at[chunk, pl.ds(0, H)], right_in.at[0, chunk, pl.ds(0, H)]
        else:
            src, dst = right_in.at[step - 1, chunk], right_in.at[step, chunk]
        return pltpu.make_async_remote_copy(
            src_ref=src, dst_ref=dst, send_sem=right_send.at[step, chunk], recv_sem=right_recv.at[step, chunk],
            device_id=(me, z_right), device_id_type=MESH)

    def left_copy(step, chunk):
        if step == 0:
            src, dst = first.at[chunk, pl.ds(H, H)], left_in.at[0, chunk, pl.ds(H, H)]
        else:
            src, dst = left_in.at[step - 1, chunk], left_in.at[step, chunk]
        return pltpu.make_async_remote_copy(
            src_ref=src, dst_ref=dst, send_sem=left_send.at[step, chunk], recv_sem=left_recv.at[step, chunk],
            device_id=(me, z_left), device_id_type=MESH)

    for distance in (3, 5, 2, 6, 1, 7, 0):
        ints_copy(lax.rem(z + distance, NZ)).start()

    own_rows = pltpu.make_async_copy(fin_out.at[0], out.at[me], load_sem.at[1])
    load_amp.wait()
    pl.semaphore_wait(barrier, NB - 1 + 2)

    spread_rows = lax.broadcasted_iota(I32, (RB, RB * TW), 0)
    spread_lanes = lax.broadcasted_iota(I32, (RB, RB * TW), 1)
    spread = jnp.where(spread_lanes // TW == spread_rows, 1.0, 0.0)

    def send_amplitudes(chunk):
        pieces = []
        for u in range(BPC):
            there = shifted(y, x, core, chunk * BPC + u, 1)
            for k in range(KV):
                hit = jnp.where(tile_lanes[pl.ds(0, 1), :] == wanted[k, pl.ds(there, 1), :], 1.0, 0.0)
                hit = jnp.concatenate([hit] * (RB * TW // 128), axis=1)
                pieces.append((spread * hit).astype(BF16))
        picked = dot(jnp.concatenate(pieces, axis=0), amp[...]).astype(BF16)
        amp_out[pl.ds(chunk * BPC, BPC)] = picked.reshape(BPC, KV, RB, W)

        @pl.when(chunk == 0)
        def _():
            amp_in[0] = picked[: KV * RB].reshape(KV, RB, W)

        for u in range(BPC):
            @pl.when(chunk * BPC + u > 0)
            def _():
                amp_copy(chunk * BPC + u).start()

    @pl.loop(0, AHEAD)
    def _(chunk):
        send_amplitudes(chunk)

    def multiply(chunk, part, store):
        def go(amount):
            total = None
            for k in range(KV):
                left = amp_in[pl.ds(chunk * BPC, amount * BPC), k].reshape(amount * R, W)
                value = dot_t(left, ints[k, part])
                total = value if total is None else total + value
            store(pl.ds(chunk, amount), total.reshape(amount, R, W))

        @pl.when(chunk == 0)
        def _():
            ints_copy(part).wait()

        @pl.when(chunk < SINGLE)
        def _():
            go(1)

        @pl.when((chunk >= SINGLE) & (chunk % 2 == 0))
        def _():
            go(2)

    def keep(index):
        def store(span, value):
            own[index, span] = value

        return store

    def keep_first(span, value):
        first[span] = value.astype(BF16)

    def arrived(chunk):
        for u in range(BPC):
            @pl.when(chunk * BPC + u > 0)
            def _():
                amp_copy(chunk * BPC + u).wait_recv()

    @pl.loop(0, NC + 4)
    def _(t):
        @pl.when(t < NC)
        def _():
            @pl.when((t < SINGLE) | (t % 2 == 0))
            def _():
                arrived(t)

            @pl.when((t >= SINGLE) & (t % 2 == 0))
            def _():
                arrived(t + 1)

            multiply(t, lax.rem(z + 4, NZ), keep_first)
            right_copy(0, t).start()
            left_copy(0, t).start()

        for step in (1, 2, 3):
            chunk = t - step

            @pl.when((chunk >= 0) & (chunk < NC))
            def _():
                at = 2 * (step - 1)
                multiply(chunk, lax.rem(z + 4 - step, NZ), keep(at))
                multiply(chunk, lax.rem(z + NZ - 4 + step, NZ), keep(at + 1))
                right_copy(step - 1, chunk).wait_recv()
                if step == 1:
                    right_in[0, chunk, :H] = (own[at, chunk, :H] + right_in[0, chunk, :H].astype(F32)).astype(BF16)
                    right_in[0, chunk, H:] = own[at, chunk, H:].astype(BF16)
                else:
                    right_in[step - 1, chunk] = (own[at, chunk] + right_in[step - 1, chunk].astype(F32)).astype(BF16)
                right_copy(step, chunk).start()
                left_copy(step - 1, chunk).wait_recv()
                if step == 1:
                    left_in[0, chunk, :H] = own[at + 1, chunk, :H].astype(BF16)
                    left_in[0, chunk, H:] = (own[at + 1, chunk, H:] + left_in[0, chunk, H:].astype(F32)).astype(BF16)
                else:
                    left_in[step - 1, chunk] = (own[at + 1, chunk] + left_in[step - 1, chunk].astype(F32)).astype(BF16)
                left_copy(step, chunk).start()

        last = t - 4

        @pl.when((last >= 0) & (last < NC))
        def _():
            multiply(last, z, keep(6))
            right_copy(3, last).wait_recv()
            left_copy(3, last).wait_recv()
            value = own[6, last] + right_in[3, last].astype(F32) + left_in[3, last].astype(F32)
            fin_out[pl.ds(last * BPC, BPC)] = value.astype(BF16).reshape(BPC, RB, W)

            @pl.when(last == 0)
            def _():
                own_rows.start()

            for u in range(BPC):
                @pl.when(last * BPC + u > 0)
                def _():
                    fin_copy(last * BPC + u).start()

        @pl.when(2 * t < NC - AHEAD)
        def _():
            send_amplitudes(AHEAD + 2 * t)
            send_amplitudes(AHEAD + 2 * t + 1)

    own_rows.wait()

    @pl.loop(1, NB)
    def _(slot):
        amp_copy(slot).wait_send()
        fin_copy(slot).wait()

    @pl.loop(0, NC)
    def _(chunk):
        for step in range(4):
            right_copy(step, chunk).wait_send()
            left_copy(step, chunk).wait_send()


def place(q_owner, rows, out, spread):
    for q in range(NB):
        block = rows[q_owner[q]].astype(F32)
        for i in range(PW // 128):
            spread[i, pl.ds(q, RB, stride=STRIDE), :] = block[:, i * 128 : (i + 1) * 128]
    for i in range(PW // 128):
        out[:, :, i * 128 : (i + 1) * 128] = spread[i].reshape(RB, STRIDE, 128)[:, :NB].astype(BF16)


def on_device(amplitudes, amp_tiles, integrals, cd_tiles, q_owner):
    any_space = pl.BlockSpec(memory_space=pl.ANY)
    smem = pl.BlockSpec(memory_space=pltpu.SMEM)
    dma = pltpu.SemaphoreType.DMA
    result = pl.pallas_call(
        kernel,
        out_shape=jax.ShapeDtypeStruct((NB, RB, W), BF16),
        in_specs=[any_space] * 5,
        out_specs=any_space,
        scratch_shapes=[
            pltpu.SMEM((TW, NB), I32),
            pltpu.SMEM((KV, NB), I32),
            pltpu.SMEM((NB,), I32),
            pltpu.VMEM((RB * TW, W), BF16),
            pltpu.VMEM((KV, NZ, W, W), BF16),
            pltpu.VMEM((KV, NB, 128), I32),
            pltpu.VMEM((8, 128), I32),
            pltpu.VMEM((NB, KV, RB, W), BF16),
            pltpu.VMEM((NB, KV, RB, W), BF16),
            pltpu.VMEM((NC, R, W), BF16),
            pltpu.VMEM((7, NC, R, W), F32),
            pltpu.VMEM((4, NC, R, W), BF16),
            pltpu.VMEM((4, NC, R, W), BF16),
            pltpu.VMEM((NB, RB, W), BF16),
            dma((5,)), dma((NZ,)), dma((NB,)), dma((NB,)),
            dma((4, NC)), dma((4, NC)), dma((4, NC)), dma((4, NC)),
            dma((NB,)), dma((NB,)),
        ],
        compiler_params=pltpu.CompilerParams(
            collective_id=0, has_side_effects=True, vmem_limit_bytes=56 * 1024 * 1024),
        name="ladder",
    )(amp_tiles.T, cd_tiles.T, q_owner, amplitudes.reshape(RB * TW, W), integrals.reshape(KV, NZ, W, W))
    return pl.pallas_call(
        place,
        out_shape=jax.ShapeDtypeStruct((RB, NB, W), BF16),
        grid=(W // PW,),
        in_specs=[smem, pl.BlockSpec((NB, RB, PW), lambda i: (0, 0, i))],
        out_specs=pl.BlockSpec((RB, NB, PW), lambda i: (0, 0, i)),
        scratch_shapes=[pltpu.VMEM((PW // 128, RB * STRIDE, 128), F32)],
        name="place",
    )(q_owner, result)


def solution(mesh):
    placed = (P("wide", None, "narrow"), P(), P("wide", None, None, "narrow"), P(), P())
    return jax.shard_map(
        on_device, mesh=mesh, in_specs=placed, out_specs=P("wide", None, "narrow"), check_vma=False
    )
```

time: 116 us -> 108 us (0.931)
  Pallas kernels: 113 us -> 108 us
  local copies, waits for them, and re-layouts: 2.3 us -> 0 us
    pallas_call x1 -> x2, Pallas kernels: 113 us -> 108 us  [the longest x1 106 us: on_device(): pl.pallas_call(kernel, out_shape=jax.ShapeDtypeStruct((NB, RB, W), BF16),...]
    unnamed x1 -> x0, local copies, waits for them, and re-layouts: 2.3 us -> none
where the time goes in v3:
time: 108 us
  Pallas kernels  108 us (100%)
    pallas_call x1, Pallas kernels, on_device(): pl.pallas_call(kernel, out_shape=jax.ShapeDtypeStruct((NB, RB, W), BF16),...  106 us
    pallas_call x1, Pallas kernels, on_device(): pl.pallas_call(place, out_shape=jax.ShapeDtypeStruct((RB, NB, W), BF16),...  2.5 us

profile of v3, /device:TPU:1, one launch (start us, length us, event | category | flops | bytes accessed | tf_op | source)
XLA Modules:
  0.0 108.1 jit_solution(17458784452838118089)
XLA Ops:
  0.0 105.5 %ladder.1.rows = bf16[32,32,512]{2,1,0:T(8,128)(2,1)} custom-call(s32[16,32]{1,0:T(8,128)} %bitcast.6, s32[2,32]{1,0:T(2,128)} %bitcast.7, s32[32]{0:T(128)} %q_owner.1, bf16[512,512]{1,0:T(8,128)(2,1)} %bitcast.5, bf16[2,8,512,512]{3,2,1,0:T(8,128)(2,1)} %bitcast.4), custom_call_target="tpu_custom_call" | custom-call | tf_op jit(solution)/shard_map/ladder/pallas_call | solution.py:297
  105.6 2.5 %place.1 = bf16[32,32,512]{2,1,0:T(8,128)(2,1)} custom-call(s32[32]{0:T(128)} %q_owner.1, bf16[32,32,512]{2,1,0:T(8,128)(2,1)} %ladder.1.rows), custom_call_target="tpu_custom_call" | custom-call | tf_op jit(solution)/shard_map/place/pallas_call | solution.py:325

commit v4 on v3

--- a/solution.py
+++ b/solution.py
@@ -138,13 +138,12 @@
 
     own_rows = pltpu.make_async_copy(fin_out.at[0], out.at[me], load_sem.at[1])
     load_amp.wait()
-    pl.semaphore_wait(barrier, NB - 1 + 2)
 
     spread_rows = lax.broadcasted_iota(I32, (RB, RB * TW), 0)
     spread_lanes = lax.broadcasted_iota(I32, (RB, RB * TW), 1)
     spread = jnp.where(spread_lanes // TW == spread_rows, 1.0, 0.0)
 
-    def send_amplitudes(chunk):
+    def pick_amplitudes(chunk):
         pieces = []
         for u in range(BPC):
             there = shifted(y, x, core, chunk * BPC + u, 1)
@@ -159,10 +158,17 @@
         def _():
             amp_in[0] = picked[: KV * RB].reshape(KV, RB, W)
 
+    def send_amplitudes(chunk):
         for u in range(BPC):
             @pl.when(chunk * BPC + u > 0)
             def _():
                 amp_copy(chunk * BPC + u).start()
+
+    @pl.loop(0, AHEAD)
+    def _(chunk):
+        pick_amplitudes(chunk)
+
+    pl.semaphore_wait(barrier, NB - 1 + 2)
 
     @pl.loop(0, AHEAD)
     def _(chunk):
@@ -264,8 +270,9 @@
 
         @pl.when(2 * t < NC - AHEAD)
         def _():
-            send_amplitudes(AHEAD + 2 * t)
-            send_amplitudes(AHEAD + 2 * t + 1)
+            for more in range(2):
+                pick_amplitudes(AHEAD + 2 * t + more)
+                send_amplitudes(AHEAD + 2 * t + more)
 
     own_rows.wait()
 

time: 108 us -> 108 us (level)
  no operation moved by 1% of the time
where the time goes in v4:
time: 108 us
  Pallas kernels  108 us (100%)
    pallas_call x1, Pallas kernels, on_device(): pl.pallas_call(kernel, out_shape=jax.ShapeDtypeStruct((NB, RB, W), BF16),...  105 us
    pallas_call x1, Pallas kernels, on_device(): pl.pallas_call(place, out_shape=jax.ShapeDtypeStruct((RB, NB, W), BF16),...  2.5 us

profile of v4, /device:TPU:1, one launch (start us, length us, event | category | flops | bytes accessed | tf_op | source)
XLA Modules:
  0.0 107.6 jit_solution(11913566643284100340)
XLA Ops:
  0.0 105.1 %ladder.1.rows = bf16[32,32,512]{2,1,0:T(8,128)(2,1)} custom-call(s32[16,32]{1,0:T(8,128)} %bitcast.6, s32[2,32]{1,0:T(2,128)} %bitcast.7, s32[32]{0:T(128)} %q_owner.1, bf16[512,512]{1,0:T(8,128)(2,1)} %bitcast.5, bf16[2,8,512,512]{3,2,1,0:T(8,128)(2,1)} %bitcast.4), custom_call_target="tpu_custom_call" | custom-call | tf_op jit(solution)/shard_map/ladder/pallas_call | solution.py:304
  105.1 2.5 %place.1 = bf16[32,32,512]{2,1,0:T(8,128)(2,1)} custom-call(s32[32]{0:T(128)} %q_owner.1, bf16[32,32,512]{2,1,0:T(8,128)(2,1)} %ladder.1.rows), custom_call_target="tpu_custom_call" | custom-call | tf_op jit(solution)/shard_map/place/pallas_call | solution.py:332

commit v5 on v4

--- a/solution.py
+++ b/solution.py
@@ -23,7 +23,7 @@
 PW = 256
 STRIDE = 40
 SX, SY = 4, 4
-AHEAD = 4
+AHEAD = 6
 SINGLE = 2
 CHIPS = [(0, 0), (0, 1), (0, 3), (1, 0), (1, 1), (3, 3), (1, 3), (3, 1), (0, 2), (2, 0), (2, 1), (2, 3), (1, 2), (3, 2), (2, 2), (3, 0)]
 

time: 108 us -> 108 us (level)
  no operation moved by 1% of the time
where the time goes in v5:
time: 108 us
  Pallas kernels  108 us (100%)
    pallas_call x1, Pallas kernels, on_device(): pl.pallas_call(kernel, out_shape=jax.ShapeDtypeStruct((NB, RB, W), BF16),...  106 us
    pallas_call x1, Pallas kernels, on_device(): pl.pallas_call(place, out_shape=jax.ShapeDtypeStruct((RB, NB, W), BF16),...  2.5 us

profile of v5, /device:TPU:1, one launch (start us, length us, event | category | flops | bytes accessed | tf_op | source)
XLA Modules:
  0.0 108.3 jit_solution(4870037505685739437)
XLA Ops:
  0.0 105.8 %ladder.1.rows = bf16[32,32,512]{2,1,0:T(8,128)(2,1)} custom-call(s32[16,32]{1,0:T(8,128)} %bitcast.6, s32[2,32]{1,0:T(2,128)} %bitcast.7, s32[32]{0:T(128)} %q_owner.1, bf16[512,512]{1,0:T(8,128)(2,1)} %bitcast.5, bf16[2,8,512,512]{3,2,1,0:T(8,128)(2,1)} %bitcast.4), custom_call_target="tpu_custom_call" | custom-call | tf_op jit(solution)/shard_map/ladder/pallas_call | solution.py:304
  105.8 2.5 %place.1 = bf16[32,32,512]{2,1,0:T(8,128)(2,1)} custom-call(s32[32]{0:T(128)} %q_owner.1, bf16[32,32,512]{2,1,0:T(8,128)(2,1)} %ladder.1.rows), custom_call_target="tpu_custom_call" | custom-call | tf_op jit(solution)/shard_map/place/pallas_call | solution.py:332
